TPU v7x, 32 devices: a whole 2x2x4 slice. The times are simulated.
32 devices in a mesh: outer: 4 (over y, x), inner: 2 (over core), col: 4 (over z).
Axes of the slice: x: 2, y: 2, z: 4, core: 2. Of those that a mesh axis runs over, the one named last changes fastest.
Arguments:
- operator: bfloat16 [4096, 8192], P(('outer', 'inner'), 'col'), as said below
- test_matrix: bfloat16 [8192, 256], P('col'), may hold values from -6 to 6
Outputs:
- basis: float32 [4096, 256], P(('outer', 'inner'), 'col')
- factor: float32 [256, 256], replicated
Inputs may be any that keep to these rules, and one draw needn't show every extreme that they name: Entries of the operator are of order 1 / sqrt(8192) times row and column scales between 0.5 and 4.
All inputs are finite; a program needn't handle non-finite values.
Results may differ from a plain program's by a relative error of at most 0.003.
Values may be sent and summed in bfloat16 or wider, within the bound.
A program may use at most 64 MiB of HBM per device.

v0:
```python
import jax
import jax.numpy as jnp
from jax import lax
from jax.sharding import PartitionSpec as P


def right_solve(lower, matrix):
    return jax.scipy.linalg.solve_triangular(lower, matrix.T, lower=True).T


def transposed_product(block, sketch):
    return lax.dot_general(
        block, sketch, (((0,), (0,)), ((), ())), preferred_element_type=jnp.float32
    )


def shards(operator, test_matrix):
    row_groups = lax.axis_size("outer") * lax.axis_size("inner")
    col_groups = lax.axis_size("col")
    local_cols = operator.shape[1]
    total_rows = operator.shape[0] * row_groups
    total_cols = local_cols * col_groups
    ratio = total_cols / total_rows
    partial_sketch = jnp.dot(operator, test_matrix, preferred_element_type=jnp.float32)
    sketch = lax.psum(partial_sketch, "col").astype(jnp.bfloat16)
    partial_normal = transposed_product(operator, sketch)
    summed = lax.psum(partial_normal, ("outer", "inner"))
    normal = (summed * ratio).astype(jnp.bfloat16)
    partial_image = jnp.dot(operator, normal, preferred_element_type=jnp.float32)
    image = lax.psum(partial_image, "col")
    local_gram = jnp.dot(
        image.T, image, precision=lax.Precision.HIGHEST, preferred_element_type=jnp.float32
    )
    gram = lax.psum(local_gram, ("outer", "inner"))
    lower = jnp.linalg.cholesky(gram)
    width = image.shape[1] // col_groups
    orthonormal = right_solve(lower, image)
    root = jnp.sqrt(jnp.float32(total_rows))
    basis = lax.dynamic_slice_in_dim(orthonormal, lax.axis_index("col") * width, width, 1) * root
    factor = lower.T / root
    return (basis, factor)


def solution(mesh):
    placed = (P(("outer", "inner"), "col"), P("col", None))
    return jax.shard_map(
        shards,
        mesh=mesh,
        in_specs=placed,
        out_specs=(P(("outer", "inner"), "col"), P()),
        check_vma=False,
    )
```

profile of v0, /device:TPU:0, one launch (start us, length us, event | category | flops | bytes accessed | tf_op | source)
XLA Modules:
  0.0 275.8 jit_solution(421812006087493749)
XLA Ops:
  7.2 0.0 copy-start
  7.2 0.0 all-reduce.6.cloned.1.call-start
  7.2 1.5 copy-done
  8.8 1.9 fusion.16
  10.7 32.1 %all-reduce.11 = bf16[512,256]{1,0:T(8,128)(2,1)S(1)} all-reduce(f32[512,256]{1,0:T(8,128)S(1)} %fusion.16), channel_id=1, replica_groups=mesh['outer'=4,'inner'=2,'col'=4] {'col'}, use_global_device_ids=true, to_apply=%region_0.0 | all-reduce | flops 131072 | bytes 786432 | tf_op jit(solution)/shard_map/psum | solution.py:25
  42.8 2.0 convolution_bitcast_fusion
  44.8 0.0 all-reduce.6.cloned.1.call-update
  44.9 0.0 all-reduce.8.cloned.1.call-start
  44.9 60.1 %all-reduce.6.cloned.1.call-done = f32[2048,256]{0,1:T(8,128)} async-done(((f32[2048,256]{0,1:T(8,128)}), f32[2048,256]{0,1:T(8,128)}) %all-reduce.6.cloned.1.call-update) | async-done | bytes 2097168 | tf_op jit(solution)/shard_map/psum | solution.py:27
  105.0 3.1 %convolution_bitcast_fusion.1 = f32[512,256]{0,1:T(8,128)} fusion(bf16[512,2048]{1,0:T(8,128)(2,1)S(1)} %copy-done, f32[2048,256]{0,1:T(8,128)} %all-reduce.6.cloned.1.call-done), kind=kOutput, calls=%fused_computation.4 | convolution fusion | flops 537919488 | bytes 4718592 | tf_op jit(solution)/shard_map/dot_general | solution.py:29
  108.1 0.0 all-reduce.8.cloned.1.call-update
  108.1 0.2 all-reduce.10.cloned.1.call-start
  108.4 37.4 %all-reduce.8.cloned.1.call-done = f32[512,256]{0,1:T(8,128)} async-done(((f32[512,256]{0,1:T(8,128)}), f32[512,256]{0,1:T(8,128)}) %all-reduce.8.cloned.1.call-update) | async-done | bytes 524304 | tf_op jit(solution)/shard_map/psum | solution.py:30
  145.8 2.5 fusion.17
  148.3 0.0 all-reduce.10.cloned.1.call-update
  148.4 0.0 copy-start.1
  148.4 54.6 %all-reduce.10.cloned.1.call-done = f32[256,256]{0,1:T(8,128)} async-done(((f32[256,256]{0,1:T(8,128)}), f32[256,256]{0,1:T(8,128)}) %all-reduce.10.cloned.1.call-update) | async-done | bytes 262160 | tf_op jit(solution)/shard_map/psum | solution.py:34
  203.0 1.1 copy.5
  204.1 1.0 fusion.3
  205.1 11.7 %cholesky.50 = f32[128,128]{1,0:T(8,128)S(1)} custom-call(f32[128,128]{1,0:T(8,128)S(1)} %cholesky.118), custom_call_target="Cholesky" | custom-call | tf_op jit(solution)/shard_map/jit(cholesky)/cholesky | solution.py:35
  216.8 9.8 %custom-call.15 = f32[1,128,128]{1,2,0:T(8,128)S(1)} custom-call(f32[1,128,128]{2,1,0:T(8,128)S(1)} %get-tuple-element.27), custom_call_target="InvertDiagBlocksLowerTriangular" | custom-call | tf_op jit(solution)/shard_map/jit(cholesky)/cholesky | solution.py:35
  226.7 0.2 constant_dynamic-update-slice_fusion
  226.9 0.3 convolution_subtract_fusion.1
  227.2 11.7 %cholesky.105 = f32[128,128]{1,0:T(8,128)S(1)} custom-call(f32[128,128]{1,0:T(8,128)S(1)} %convolution_subtract_fusion.1), custom_call_target="Cholesky" | custom-call | tf_op jit(solution)/shard_map/jit(cholesky)/cholesky | solution.py:35
  238.9 0.7 compare_reduce_fusion
  241.0 0.1 triangular_solve.57
  241.1 4.3 %while.1 = (s32[]{:T(128)}, f32[256,256]{1,0:T(8,128)S(1)}, s32[2,2]{1,0:T(2,128)S(1)}, f32[2,128,128]{2,1,0:T(8,128)S(1)}, s32[]{:T(128)}) while((s32[]{:T(128)}, f32[256,256]{1,0:T(8,128)S(1)}, s32[2,2]{1,0:T(2,128)S(1)}, f32[2,128,128]{2,1,0:T(8,128)S(1)}, s32[]{:T(128)}) %tuple.29), condition=%wide.while_cond, body=%wide.while_body.sunk | while | flops 2 | bytes 131181 | solution.py:8
  241.3 0.6 fusion.30
  241.9 1.4 bitcast_dynamic-update-slice_fusion.2
  243.3 0.6 fusion.30
  243.9 1.4 bitcast_dynamic-update-slice_fusion.2
  245.4 0.0 copy-start.2
  245.4 0.6 copy-done.2
  246.0 20.5 %custom-call.16 = f32[2,128,128]{1,2,0:T(8,128)S(1)} custom-call(f32[2,128,128]{2,1,0:T(8,128)} %copy-done.2), custom_call_target="InvertDiagBlocksLowerTriangular" | custom-call | tf_op jit(solution)/shard_map/jit(_solve_triangular)/triangular_solve | solution.py:8
  266.5 0.0 copy-done.1
  266.5 0.4 fusion.1
  267.0 0.4 convolution_subtract_fusion
  267.3 0.4 fusion.10
  267.8 0.8 copy.6
  268.6 0.7 fusion.8
  (9 shorter events, 0.2 us)
Async XLA Ops:
  7.2 1.6 copy-start
  7.2 97.8 %all-reduce.6.cloned.1.call-start = ((), (), s32[]{:S(2)}) async-start(), calls=%async_computation | async-start | bytes 4194304 | tf_op jit(solution)/shard_map/psum | solution.py:27
  44.9 101.0 %all-reduce.8.cloned.1.call-start = ((), (), s32[]{:S(2)}) async-start(), calls=%async_computation.1 | async-start | bytes 1048576 | tf_op jit(solution)/shard_map/psum | solution.py:30
  108.1 94.8 %all-reduce.10.cloned.1.call-start = ((), (), s32[]{:S(2)}) async-start(), calls=%async_computation.2 | async-start | bytes 524288 | tf_op jit(solution)/shard_map/psum | solution.py:34
  148.4 118.2 %copy-start.1 = (f32[512,256]{0,1:T(8,128)S(1)}, f32[512,256]{0,1:T(8,128)}, u32[]{:S(2)}) copy-start(f32[512,256]{0,1:T(8,128)} %all-reduce.8.cloned.1.call-done) | copy-start | bytes 1572868
  245.4 0.7 copy-start.2
Sparse Core Ops, SparseCore 0:
  45.0 59.9 all-reduce.5
  108.3 37.4 all-reduce.7
  149.4 53.5 all-reduce.9
where the time goes:
time: 276 us
  waiting for transfers between devices  152 us (55%)
  other arithmetic  56.2 us (20%)
  blocking collectives  32.1 us (12%)
  between operations  15.2 us (6%)
  matrix products  11.3 us (4%)
  local copies, waits for them, and re-layouts  8.27 us (3%)
    psum x1, waiting for transfers between devices, shards(): summed = lax.psum(partial_normal, ('outer', 'inner'))  60.1 us
    psum x1, waiting for transfers between devices, shards(): gram = lax.psum(local_gram, ('outer', 'inner'))  54.6 us
    psum x1, waiting for transfers between devices, shards(): image = lax.psum(partial_image, 'col')  37.4 us
    another operation x6, other arithmetic, shards(): lower = jnp.linalg.cholesky(gram)  34 us
    psum x1, blocking collectives, shards(): sketch = lax.psum(partial_sketch, 'col').astype(jnp.bfloat16)  32.1 us
    another operation x2, other arithmetic, right_solve(): return jax.scipy.linalg.solve_triangular(lower, matrix.T, lower=True).T  20.5 us
  transfers between devices with their start and end apart: 3, of which 3 were waited for; matrix products, arithmetic and copies ran while one was open for 0% of the time, Pallas kernels for 0%

commit v1 on v0

--- a/solution.py
+++ b/solution.py
@@ -31,7 +31,7 @@
     local_gram = jnp.dot(
         image.T, image, precision=lax.Precision.HIGHEST, preferred_element_type=jnp.float32
     )
-    gram = lax.psum(local_gram, ("outer", "inner"))
+    gram = lax.psum(lax.psum(local_gram, "inner"), "outer")
     lower = jnp.linalg.cholesky(gram)
     width = image.shape[1] // col_groups
     orthonormal = right_solve(lower, image)

time: 276 us -> 287 us (1.040)
  waiting for transfers between devices: 152 us -> 163 us
    psum x1 -> x2, waiting for transfers between devices: 54.6 us -> 65.5 us  [shards(): gram = lax.psum(lax.psum(local_gram, 'inner'), 'outer')]
  transfers between devices with their start and end apart: 3 -> 4, of which waited for: 3 -> 4; matrix products, arithmetic and copies ran while one was open for 0% -> 0% of each run, Pallas kernels for 0% -> 0%
where the time goes in v1:
time: 287 us
  waiting for transfers between devices  163 us (57%)
  other arithmetic  56.2 us (20%)
  blocking collectives  32.1 us (11%)
  between operations  15.3 us (5%)
  matrix products  11.3 us (4%)
  local copies, waits for them, and re-layouts  8.27 us (3%)
    psum x2, waiting for transfers between devices, shards(): gram = lax.psum(lax.psum(local_gram, 'inner'), 'outer')  65.5 us
    psum x1, waiting for transfers between devices, shards(): summed = lax.psum(partial_normal, ('outer', 'inner'))  60.1 us
    psum x1, waiting for transfers between devices, shards(): image = lax.psum(partial_image, 'col')  37.6 us
    another operation x6, other arithmetic, shards(): lower = jnp.linalg.cholesky(gram)  34 us
    psum x1, blocking collectives, shards(): sketch = lax.psum(partial_sketch, 'col').astype(jnp.bfloat16)  32.1 us
    another operation x2, other arithmetic, right_solve(): return jax.scipy.linalg.solve_triangular(lower, matrix.T, lower=True).T  20.5 us
  transfers between devices with their start and end apart: 4, of which 4 were waited for; matrix products, arithmetic and copies ran while one was open for 0% of the time, Pallas kernels for 0%

profile of v1, /device:TPU:0, one launch (start us, length us, event | category | flops | bytes accessed | tf_op | source)
XLA Modules:
  0.0 287.0 jit_solution(14873162181937112885)
XLA Ops:
  7.2 0.0 copy-start
  7.2 0.0 all-reduce.7.cloned.1.call-start
  7.2 1.5 copy-done
  8.8 1.9 fusion.16
  10.7 32.1 %all-reduce.14 = bf16[512,256]{1,0:T(8,128)(2,1)S(1)} all-reduce(f32[512,256]{1,0:T(8,128)S(1)} %fusion.16), channel_id=1, replica_groups=mesh['outer'=4,'inner'=2,'col'=4] {'col'}, use_global_device_ids=true, to_apply=%region_0.0 | all-reduce | flops 131072 | bytes 786432 | tf_op jit(solution)/shard_map/psum | solution.py:25
  42.8 2.0 convolution_bitcast_fusion
  44.8 0.0 all-reduce.7.cloned.1.call-update
  44.9 0.0 all-reduce.9.cloned.1.call-start
  44.9 60.1 %all-reduce.7.cloned.1.call-done = f32[2048,256]{0,1:T(8,128)} async-done(((f32[2048,256]{0,1:T(8,128)}), f32[2048,256]{0,1:T(8,128)}) %all-reduce.7.cloned.1.call-update) | async-done | bytes 2097168 | tf_op jit(solution)/shard_map/psum | solution.py:27
  105.0 3.1 %convolution_bitcast_fusion.1 = f32[512,256]{0,1:T(8,128)} fusion(bf16[512,2048]{1,0:T(8,128)(2,1)S(1)} %copy-done, f32[2048,256]{0,1:T(8,128)} %all-reduce.7.cloned.1.call-done), kind=kOutput, calls=%fused_computation.4 | convolution fusion | flops 537919488 | bytes 4718592 | tf_op jit(solution)/shard_map/dot_general | solution.py:29
  108.1 0.0 all-reduce.9.cloned.1.call-update
  108.1 0.0 all-reduce.11.cloned.1.call-start
  108.2 37.6 %all-reduce.9.cloned.1.call-done = f32[512,256]{0,1:T(8,128)} async-done(((f32[512,256]{0,1:T(8,128)}), f32[512,256]{0,1:T(8,128)}) %all-reduce.9.cloned.1.call-update) | async-done | bytes 524304 | tf_op jit(solution)/shard_map/psum | solution.py:30
  145.8 2.5 fusion.17
  148.3 0.0 all-reduce.11.cloned.1.call-update
  148.3 0.2 all-reduce.13.cloned.1.call-start
  148.6 18.4 %all-reduce.11.cloned.1.call-done = f32[256,256]{0,1:T(8,128)} async-done(((f32[256,256]{0,1:T(8,128)}), f32[256,256]{0,1:T(8,128)}) %all-reduce.11.cloned.1.call-update) | async-done | bytes 262160 | tf_op jit(solution)/shard_map/psum | solution.py:34
  167.0 0.0 all-reduce.13.cloned.1.call-update
  167.0 0.0 copy-start.1
  167.0 47.1 %all-reduce.13.cloned.1.call-done = f32[256,256]{0,1:T(8,128)} async-done(((f32[256,256]{0,1:T(8,128)}), f32[256,256]{0,1:T(8,128)}) %all-reduce.13.cloned.1.call-update) | async-done | bytes 262160 | tf_op jit(solution)/shard_map/psum | solution.py:34
  214.2 1.1 copy.5
  215.2 1.0 fusion.3
  216.2 11.7 %cholesky.50 = f32[128,128]{1,0:T(8,128)S(1)} custom-call(f32[128,128]{1,0:T(8,128)S(1)} %cholesky.118), custom_call_target="Cholesky" | custom-call | tf_op jit(solution)/shard_map/jit(cholesky)/cholesky | solution.py:35
  228.0 9.8 %custom-call.15 = f32[1,128,128]{1,2,0:T(8,128)S(1)} custom-call(f32[1,128,128]{2,1,0:T(8,128)S(1)} %get-tuple-element.27), custom_call_target="InvertDiagBlocksLowerTriangular" | custom-call | tf_op jit(solution)/shard_map/jit(cholesky)/cholesky | solution.py:35
  237.8 0.2 constant_dynamic-update-slice_fusion
  238.0 0.3 convolution_subtract_fusion.1
  238.3 11.7 %cholesky.105 = f32[128,128]{1,0:T(8,128)S(1)} custom-call(f32[128,128]{1,0:T(8,128)S(1)} %convolution_subtract_fusion.1), custom_call_target="Cholesky" | custom-call | tf_op jit(solution)/shard_map/jit(cholesky)/cholesky | solution.py:35
  250.1 0.7 compare_reduce_fusion
  252.2 0.1 triangular_solve.57
  252.3 4.3 %while.1 = (s32[]{:T(128)}, f32[256,256]{1,0:T(8,128)S(1)}, s32[2,2]{1,0:T(2,128)S(1)}, f32[2,128,128]{2,1,0:T(8,128)S(1)}, s32[]{:T(128)}) while((s32[]{:T(128)}, f32[256,256]{1,0:T(8,128)S(1)}, s32[2,2]{1,0:T(2,128)S(1)}, f32[2,128,128]{2,1,0:T(8,128)S(1)}, s32[]{:T(128)}) %tuple.29), condition=%wide.while_cond, body=%wide.while_body.sunk | while | flops 2 | bytes 131181 | solution.py:8
  252.4 0.6 fusion.30
  253.0 1.4 bitcast_dynamic-update-slice_fusion.2
  254.5 0.6 fusion.30
  255.1 1.4 bitcast_dynamic-update-slice_fusion.2
  256.5 0.0 copy-start.2
  256.6 0.6 copy-done.2
  257.2 20.5 %custom-call.16 = f32[2,128,128]{1,2,0:T(8,128)S(1)} custom-call(f32[2,128,128]{2,1,0:T(8,128)} %copy-done.2), custom_call_target="InvertDiagBlocksLowerTriangular" | custom-call | tf_op jit(solution)/shard_map/jit(_solve_triangular)/triangular_solve | solution.py:8
  277.7 0.0 copy-done.1
  277.7 0.4 fusion.1
  278.1 0.4 convolution_subtract_fusion
  278.5 0.4 fusion.10
  278.9 0.8 copy.6
  279.8 0.7 fusion.8
  (9 shorter events, 0.2 us)
Async XLA Ops:
  7.2 1.6 copy-start
  7.2 97.8 %all-reduce.7.cloned.1.call-start = ((), (), s32[]{:S(2)}) async-start(), calls=%async_computation | async-start | bytes 4194304 | tf_op jit(solution)/shard_map/psum | solution.py:27
  44.9 101.0 %all-reduce.9.cloned.1.call-start = ((), (), s32[]{:S(2)}) async-start(), calls=%async_computation.1 | async-start | bytes 1048576 | tf_op jit(solution)/shard_map/psum | solution.py:30
  108.1 58.8 %all-reduce.11.cloned.1.call-start = ((), (), s32[]{:S(2)}) async-start(), calls=%async_computation.2 | async-start | bytes 524288 | tf_op jit(solution)/shard_map/psum | solution.py:34
  148.3 65.8 %all-reduce.13.cloned.1.call-start = ((), (), s32[]{:S(2)}) async-start(), calls=%async_computation.3 | async-start | bytes 524288 | tf_op jit(solution)/shard_map/psum | solution.py:34
  167.0 110.7 %copy-start.1 = (f32[512,256]{0,1:T(8,128)S(1)}, f32[512,256]{0,1:T(8,128)}, u32[]{:S(2)}) copy-start(f32[512,256]{0,1:T(8,128)} %all-reduce.9.cloned.1.call-done) | copy-start | bytes 1572868
  256.5 0.7 copy-start.2
Sparse Core Ops, SparseCore 0:
  45.0 59.9 all-reduce.6
  108.3 37.4 all-reduce.8
  148.7 18.2 all-reduce.10
  170.0 44.0 all-reduce.12

commit v2 on v0

--- a/solution.py
+++ b/solution.py
@@ -31,7 +31,7 @@
     local_gram = jnp.dot(
         image.T, image, precision=lax.Precision.HIGHEST, preferred_element_type=jnp.float32
     )
-    gram = lax.psum(local_gram, ("outer", "inner"))
+    gram = jnp.sum(lax.all_gather(local_gram, ("outer", "inner")), axis=0)
     lower = jnp.linalg.cholesky(gram)
     width = image.shape[1] // col_groups
     orthonormal = right_solve(lower, image)

time: 276 us -> 249 us (0.902)
  waiting for transfers between devices: 152 us -> 126 us
    psum x1 -> x0, waiting for transfers between devices: 54.6 us -> none  [shards(): gram = lax.psum(local_gram, ('outer', 'inner'))]
    all_gather x0 -> x1, waiting for transfers between devices: none -> 28 us  [shards(): gram = jnp.sum(lax.all_gather(local_gram, ('outer', 'inner')), axis=0)]
where the time goes in v2:
time: 249 us
  waiting for transfers between devices  126 us (51%)
  other arithmetic  57 us (23%)
  blocking collectives  32.1 us (13%)
  between operations  15.3 us (6%)
  matrix products  11.3 us (5%)
  local copies, waits for them, and re-layouts  7.32 us (3%)
    psum x1, waiting for transfers between devices, shards(): summed = lax.psum(partial_normal, ('outer', 'inner'))  60.1 us
    psum x1, waiting for transfers between devices, shards(): image = lax.psum(partial_image, 'col')  37.4 us
    another operation x6, other arithmetic, shards(): lower = jnp.linalg.cholesky(gram)  34 us
    psum x1, blocking collectives, shards(): sketch = lax.psum(partial_sketch, 'col').astype(jnp.bfloat16)  32.1 us
    all_gather x1, waiting for transfers between devices, shards(): gram = jnp.sum(lax.all_gather(local_gram, ('outer', 'inner')), axis=0)  28 us
    another operation x2, other arithmetic, right_solve(): return jax.scipy.linalg.solve_triangular(lower, matrix.T, lower=True).T  20.5 us
  transfers between devices with their start and end apart: 3, of which 3 were waited for; matrix products, arithmetic and copies ran while one was open for 0% of the time, Pallas kernels for 0%

profile of v2, /device:TPU:0, one launch (start us, length us, event | category | flops | bytes accessed | tf_op | source)
XLA Modules:
  0.0 249.1 jit_solution(74896798430342276)
XLA Ops:
  7.2 0.0 copy-start
  7.2 0.0 all-reduce.5.cloned.1.call-start
  7.2 1.5 copy-done
  8.8 1.9 fusion.16
  10.7 32.1 %all-reduce.8 = bf16[512,256]{1,0:T(8,128)(2,1)S(1)} all-reduce(f32[512,256]{1,0:T(8,128)S(1)} %fusion.16), channel_id=1, replica_groups=mesh['outer'=4,'inner'=2,'col'=4] {'col'}, use_global_device_ids=true, to_apply=%region_0.0 | all-reduce | flops 131072 | bytes 786432 | tf_op jit(solution)/shard_map/psum | solution.py:25
  42.8 2.0 convolution_bitcast_fusion
  44.8 0.0 all-reduce.5.cloned.1.call-update
  44.9 0.0 all-reduce.7.cloned.1.call-start
  44.9 60.1 %all-reduce.5.cloned.1.call-done = f32[2048,256]{0,1:T(8,128)} async-done(((f32[2048,256]{0,1:T(8,128)}), f32[2048,256]{0,1:T(8,128)}) %all-reduce.5.cloned.1.call-update) | async-done | bytes 2097168 | tf_op jit(solution)/shard_map/psum | solution.py:27
  105.0 3.2 %convolution_bitcast_fusion.1 = f32[512,256]{0,1:T(8,128)} fusion(bf16[512,2048]{1,0:T(8,128)(2,1)S(1)} %copy-done, f32[2048,256]{0,1:T(8,128)} %all-reduce.5.cloned.1.call-done), kind=kOutput, calls=%fused_computation.4 | convolution fusion | flops 537919488 | bytes 4718592 | tf_op jit(solution)/shard_map/dot_general | solution.py:29
  108.1 0.0 all-reduce.7.cloned.1.call-update
  108.2 0.2 all-gather.3.cloned.1.call-start
  108.4 37.4 %all-reduce.7.cloned.1.call-done = f32[512,256]{0,1:T(8,128)} async-done(((f32[512,256]{0,1:T(8,128)}), f32[512,256]{0,1:T(8,128)}) %all-reduce.7.cloned.1.call-update) | async-done | bytes 524304 | tf_op jit(solution)/shard_map/psum | solution.py:30
  145.8 2.5 %fusion.17 = f32[256,256]{1,0:T(8,128)} fusion(f32[512,256]{0,1:T(8,128)} %all-reduce.7.cloned.1.call-done), kind=kOutput, calls=%fused_computation.42 | convolution fusion | flops 402653184 | bytes 786432 | tf_op jit(solution)/shard_map/dot_general | solution.py:31
  148.3 0.0 all-gather.3.cloned.1.call-update
  148.4 28.0 %all-gather.3.cloned.1.call-done = f32[2048,256]{1,0:T(8,128)} async-done(((f32[256,256]{1,0:T(8,128)}), f32[2048,256]{1,0:T(8,128)}) %all-gather.3.cloned.1.call-update) | async-done | bytes 2097168 | tf_op jit(solution)/shard_map/all_gather | solution.py:34
  176.4 1.8 reduce_sum.9
  178.2 0.0 copy-start.1
  178.2 0.1 copy.6
  178.4 11.7 %cholesky.50 = f32[128,128]{1,0:T(8,128)S(1)} custom-call(f32[128,128]{1,0:T(8,128)S(1)} %cholesky.118), custom_call_target="Cholesky" | custom-call | tf_op jit(solution)/shard_map/jit(cholesky)/cholesky | solution.py:35
  190.1 9.8 %custom-call.15 = f32[1,128,128]{1,2,0:T(8,128)S(1)} custom-call(f32[1,128,128]{2,1,0:T(8,128)S(1)} %get-tuple-element.29), custom_call_target="InvertDiagBlocksLowerTriangular" | custom-call | tf_op jit(solution)/shard_map/jit(cholesky)/cholesky | solution.py:35
  200.0 0.2 constant_dynamic-update-slice_fusion
  200.2 0.3 convolution_subtract_fusion.1
  200.4 11.7 %cholesky.105 = f32[128,128]{1,0:T(8,128)S(1)} custom-call(f32[128,128]{1,0:T(8,128)S(1)} %convolution_subtract_fusion.1), custom_call_target="Cholesky" | custom-call | tf_op jit(solution)/shard_map/jit(cholesky)/cholesky | solution.py:35
  212.2 0.7 compare_reduce_fusion
  214.3 0.1 triangular_solve.57
  214.4 4.3 %while.1 = (s32[]{:T(128)}, f32[256,256]{1,0:T(8,128)S(1)}, s32[2,2]{1,0:T(2,128)S(1)}, f32[2,128,128]{2,1,0:T(8,128)S(1)}, s32[]{:T(128)}) while((s32[]{:T(128)}, f32[256,256]{1,0:T(8,128)S(1)}, s32[2,2]{1,0:T(2,128)S(1)}, f32[2,128,128]{2,1,0:T(8,128)S(1)}, s32[]{:T(128)}) %tuple.30), condition=%wide.while_cond, body=%wide.while_body.sunk | while | flops 2 | bytes 131181 | solution.py:8
  214.6 0.6 fusion.30
  215.2 1.4 bitcast_dynamic-update-slice_fusion.2
  216.6 0.6 fusion.30
  217.2 1.4 bitcast_dynamic-update-slice_fusion.2
  218.6 0.0 copy-start.2
  218.7 0.6 copy-done.2
  219.3 20.5 %custom-call.16 = f32[2,128,128]{1,2,0:T(8,128)S(1)} custom-call(f32[2,128,128]{2,1,0:T(8,128)} %copy-done.2), custom_call_target="InvertDiagBlocksLowerTriangular" | custom-call | tf_op jit(solution)/shard_map/jit(_solve_triangular)/triangular_solve | solution.py:8
  239.8 0.0 copy-done.1
  239.8 0.4 fusion.1
  240.2 0.4 convolution_subtract_fusion
  240.6 0.4 fusion.10
  241.0 0.8 copy.7
  241.9 0.7 fusion.8
  (10 shorter events, 0.2 us)
Async XLA Ops:
  7.2 1.6 copy-start
  7.2 97.8 %all-reduce.5.cloned.1.call-start = ((), (), s32[]{:S(2)}) async-start(), calls=%async_computation | async-start | bytes 4194304 | tf_op jit(solution)/shard_map/psum | solution.py:27
  44.9 101.0 %all-reduce.7.cloned.1.call-start = ((), (), s32[]{:S(2)}) async-start(), calls=%async_computation.1 | async-start | bytes 1048576 | tf_op jit(solution)/shard_map/psum | solution.py:30
  108.2 68.2 %all-gather.3.cloned.1.call-start = ((), (), s32[]{:S(2)}) async-start(), calls=%async_computation.2 | async-start | bytes 2359296 | tf_op jit(solution)/shard_map/all_gather | solution.py:34
  178.2 61.6 %copy-start.1 = (f32[512,256]{0,1:T(8,128)S(1)}, f32[512,256]{0,1:T(8,128)}, u32[]{:S(2)}) copy-start(f32[512,256]{0,1:T(8,128)} %all-reduce.7.cloned.1.call-done) | copy-start | bytes 1572868
  218.6 0.7 copy-start.2
Sparse Core Ops, SparseCore 0:
  45.0 59.9 all-reduce.4
  108.3 37.4 all-reduce.6
  148.5 27.8 all-gather.2
